TPU v7x, 32 devices: a whole 2x2x4 slice. The times are simulated.
32 devices in a mesh: row: 8 (over y, x, core), col: 4 (over z).
Axes of the slice: x: 2, y: 2, z: 4, core: 2. Of those that a mesh axis runs over, the one named last changes fastest.
Arguments:
- tokens: bfloat16 [65536, 1024], P('row', 'col'), may hold values from -6 to 6
- up_weight: bfloat16 [1024, 4096], P('row', 'col'), may hold values from -0.1875 to 0.1875
- hidden_grad: bfloat16 [65536, 4096], P('row', 'col'), may hold values from -6 to 6
Outputs:
- hidden: bfloat16 [65536, 4096], P('row', 'col')
- input_grad: bfloat16 [65536, 1024], P('row', 'col')
All inputs are finite; a program needn't handle non-finite values.
Results may differ from a plain program's by a relative error of at most 0.017.
Values may be sent and summed in bfloat16 or wider, within the bound.
No kernel may reach another device: no remote copies, remote signals or barrier semaphores. Data moves between devices by JAX's collectives and lax.ppermute only.
A program may use at most 128 MiB of HBM per device.

v0:
```python
import jax
import jax.numpy as jnp
from jax import lax
from jax.sharding import PartitionSpec as P

gelu_c = 0.7978845608028654
gelu_a = 0.044715


def gelu_value(v):
    inner = gelu_c * (v + gelu_a * v * v * v)
    return 0.5 * v * (1.0 + jnp.tanh(inner))


def gelu_slope(v):
    inner = gelu_c * (v + gelu_a * v * v * v)
    tval = jnp.tanh(inner)
    return 0.5 * (1.0 + tval) + 0.5 * v * (1.0 - tval * tval) * gelu_c * (
        1.0 + 3.0 * gelu_a * v * v
    )


def per_device(tokens, up_weight, hidden_grad):
    column_panel = lax.all_gather(up_weight, "row", axis=0, tiled=True)
    token_rows = lax.all_gather(tokens, "col", axis=1, tiled=True)
    preact = jnp.dot(token_rows, column_panel, preferred_element_type=jnp.float32)
    hidden = gelu_value(preact).astype(jnp.bfloat16)
    pre_grad = (hidden_grad.astype(jnp.float32) * gelu_slope(preact)).astype(jnp.bfloat16)
    summed = lax.psum_scatter(
        lax.dot_general(
            column_panel, pre_grad, (((1,), (1,)), ((), ())), preferred_element_type=jnp.float32
        ).astype(jnp.bfloat16),
        "col",
        scatter_dimension=0,
        tiled=True,
    ).astype(jnp.float32)
    input_grad = jnp.transpose(summed).astype(jnp.bfloat16)
    return (hidden, input_grad)


def solution(mesh):
    in_specs = (P("row", "col"), P("row", "col"), P("row", "col"))
    out_specs = (P("row", "col"), P("row", "col"))
    return jax.shard_map(
        per_device, mesh=mesh, in_specs=in_specs, out_specs=out_specs, check_vma=False
    )
```

profile of v0, /device:TPU:0, one launch (start us, length us, event | category | flops | bytes accessed | tf_op | source)
XLA Modules:
  0.0 688.1 jit_solution(10581565400900481184)
XLA Ops:
  7.2 0.0 all-gather.5.cloned.1.call-start
  7.2 0.7 all-gather.5.cloned.1.call-update
  7.9 0.0 all-gather.3.cloned.1.call-start
  7.9 0.7 all-gather.3.cloned.1.call-update
  8.6 0.0 reduce-scatter.2.cloned.1.call-start
  8.7 31.7 %all-gather.5.cloned.1.call-done = bf16[1024,1024]{1,0:T(8,128)(2,1)} async-done(((bf16[128,1024]{1,0:T(8,128)(2,1)}), bf16[1024,1024]{1,0:T(8,128)(2,1)}) %all-gather.5.cloned.1.call-update) | async-done | bytes 2097168 | tf_op jit(solution)/shard_map/all_gather | solution.py:24
  40.4 0.0 copy-start
  40.4 287.8 %all-gather.3.cloned.1.call-done = bf16[8192,1024]{1,0:T(8,128)(2,1)} async-done(((bf16[8192,256]{1,0:T(8,128)(2,1)}), bf16[8192,1024]{1,0:T(8,128)(2,1)}) %all-gather.3.cloned.1.call-update) | async-done | bytes 16777232 | tf_op jit(solution)/shard_map/all_gather | solution.py:25
  328.2 34.3 %multiply_convert_fusion = (bf16[8192,1024]{1,0:T(8,128)(2,1)}, f32[8192,1024]{1,0:T(8,128)}) fusion(bf16[8192,1024]{1,0:T(8,128)(2,1)} %all-gather.3.cloned.1.call-done, bf16[1024,1024]{1,0:T(8,128)(2,1)} %all-gather.5.cloned.1.call-done), kind=kOutput, calls=%fused_computation.9 | convolution fusion | flops 17255366656 | bytes 69206016 | tf_op jit(solution)/shard_map/dot_general | solution.py:26
  362.6 0.0 copy-done
  362.6 40.1 %convert_bitcast_fusion = bf16[1024,8192]{0,1:T(8,128)(2,1)} fusion(bf16[1024,1024]{1,0:T(8,128)(2,1)S(1)} %copy-done, f32[8192,1024]{1,0:T(8,128)} %get-tuple-element.3, bf16[8192,1024]{1,0:T(8,128)(2,1)} %param.5), kind=kOutput, calls=%fused_computation.10 | convolution fusion | flops 17356029952 | bytes 69206016 | tf_op jit(solution)/shard_map/dot_general | solution.py:30
  402.7 0.0 reduce-scatter.2.cloned.1.call-update
  402.7 278.8 %reduce-scatter.2.cloned.1.call-done = bf16[256,8192]{0,1:T(8,128)(2,1)} async-done(((bf16[1024,8192]{0,1:T(8,128)(2,1)}), bf16[256,8192]{0,1:T(8,128)(2,1)}) %reduce-scatter.2.cloned.1.call-update) | async-done | bytes 4194320 | tf_op jit(solution)/shard_map/reduce_scatter | solution.py:29
Async XLA Ops:
  7.2 33.2 %all-gather.5.cloned.1.call-start = ((), (), s32[]{:S(2)}) async-start(), calls=%async_computation.2 | async-start | bytes 2359296 | tf_op jit(solution)/shard_map/all_gather | solution.py:24
  7.9 320.3 %all-gather.3.cloned.1.call-start = ((), (), s32[]{:S(2)}) async-start(), calls=%async_computation.1 | async-start | bytes 20971520 | tf_op jit(solution)/shard_map/all_gather | solution.py:25
  8.6 672.9 %reduce-scatter.2.cloned.1.call-start = ((), (), s32[]{:S(2)}) async-start(), calls=%async_computation.3 | async-start | bytes 20971520 | tf_op jit(solution)/shard_map/reduce_scatter | solution.py:29
  40.4 322.2 %copy-start = (bf16[1024,1024]{1,0:T(8,128)(2,1)S(1)}, bf16[1024,1024]{1,0:T(8,128)(2,1)}, u32[]{:S(2)}) copy-start(bf16[1024,1024]{1,0:T(8,128)(2,1)} %all-gather.5.cloned.1.call-done) | copy-start | bytes 6291460
Sparse Core Ops, SparseCore 0:
  9.9 30.4 all-gather.4
  41.9 286.2 all-gather.2
  402.9 278.6 reduce-scatter.1
where the time goes:
time: 688 us
  waiting for transfers between devices  600 us (87%)
  matrix products  74.5 us (11%)
  between operations  13.7 us (2%)
    all_gather x1, waiting for transfers between devices, per_device(): token_rows = lax.all_gather(tokens, 'col', axis=1, tiled=True)  288 us
    reduce_scatter x1, waiting for transfers between devices, per_device(): lax.psum_scatter(lax.dot_general(column_panel, pre_grad, (((1,), (1,)), (...  279 us
    dot_general x1, matrix products, per_device(): lax.dot_general(column_panel, pre_grad, (((1,), (1,)), ((), ())), preferr...  40.1 us
    dot_general x1, matrix products, per_device(): jnp.dot(token_rows, column_panel, preferred_element_type=jnp.float32)  34.3 us
    all_gather x1, waiting for transfers between devices, per_device(): column_panel = lax.all_gather(up_weight, 'row', axis=0, tiled=True)  31.7 us
  transfers between devices with their start and end apart: 3, of which 3 were waited for; matrix products, arithmetic and copies ran while one was open for 0% of the time, Pallas kernels for 0%

commit v1 on v0

--- a/solution.py
+++ b/solution.py
@@ -21,8 +21,21 @@
 
 
 def per_device(tokens, up_weight, hidden_grad):
+
+    def _assign_halves(piece_in):
+        mesh_ax = "col"
+        full_n = lax.psum(1, mesh_ax)
+        work_now = sorted(((it, (it + 1) % full_n) for it in range(full_n)))
+        wide_out = piece_in
+        found = [wide_out]
+        for tick in range(1, full_n):
+            wide_out = lax.ppermute(wide_out, mesh_ax, work_now)
+            found.insert(0, wide_out)
+        k_now = jnp.concatenate(found, 1)
+        return jnp.roll(k_now, (lax.axis_index(mesh_ax) + 1) * piece_in.shape[1], 1)
+
     column_panel = lax.all_gather(up_weight, "row", axis=0, tiled=True)
-    token_rows = lax.all_gather(tokens, "col", axis=1, tiled=True)
+    token_rows = _assign_halves(tokens)
     preact = jnp.dot(token_rows, column_panel, preferred_element_type=jnp.float32)
     hidden = gelu_value(preact).astype(jnp.bfloat16)
     pre_grad = (hidden_grad.astype(jnp.float32) * gelu_slope(preact)).astype(jnp.bfloat16)

time: 688 us -> 684 us (level)
  waiting for transfers between devices: 600 us -> 558 us
  local copies, waits for them, and re-layouts: 0.01 us -> 33.7 us
    all_gather x1 -> x0, waiting for transfers between devices: 288 us -> none  [per_device(): token_rows = lax.all_gather(tokens, 'col', axis=1, tiled=True)]
    ppermute x0 -> x3, waiting for transfers between devices: none -> 279 us  [_assign_halves(): wide_out = lax.ppermute(wide_out, mesh_ax, work_now)]
    all_gather x1, waiting for transfers between devices: 31.7 us -> 0.01 us  [per_device(): column_panel = lax.all_gather(up_weight, 'row', axis=0, tiled=True)]
    unnamed x2 -> x15, local copies, waits for them, and re-layouts: 0.01 us -> 31.4 us
  transfers between devices with their start and end apart: 3 -> 5, of which waited for: 3 -> 4; matrix products, arithmetic and copies ran while one was open for 0% -> 5% of each run, Pallas kernels for 0% -> 0%
where the time goes in v1:
time: 684 us; the launch traced here: 683 us
  waiting for transfers between devices  558 us (82%)
  matrix products  74.7 us (11%)
  local copies, waits for them, and re-layouts  33.7 us (5%)
  between operations  14.1 us (2%)
    ppermute x3, waiting for transfers between devices, _assign_halves(): wide_out = lax.ppermute(wide_out, mesh_ax, work_now)  279 us
    reduce_scatter x1, waiting for transfers between devices, per_device(): lax.psum_scatter(lax.dot_general(column_panel, pre_grad, (((1,), (1,)), (...  278 us
    dot_general x1, matrix products, per_device(): lax.dot_general(column_panel, pre_grad, (((1,), (1,)), ((), ())), preferr...  40.2 us
    dot_general x1, matrix products, per_device(): jnp.dot(token_rows, column_panel, preferred_element_type=jnp.float32)  34.5 us
    unnamed x15, local copies, waits for them, and re-layouts  31.4 us
  transfers between devices with their start and end apart: 5, of which 4 were waited for; matrix products, arithmetic and copies ran while one was open for 5% of the time, Pallas kernels for 0%

profile of v1, /device:TPU:0, one launch (start us, length us, event | category | flops | bytes accessed | tf_op | source)
XLA Modules:
  0.0 683.3 jit_solution(2086517579136424659)
XLA Ops:
  7.2 0.0 all-gather.2.cloned.1.call-start
  7.2 3.1 collective-permute-start
  10.3 92.8 %collective-permute-done = bf16[8192,256]{1,0:T(8,128)(2,1)S(1)} collective-permute-done((bf16[8192,256]{1,0:T(8,128)(2,1)}, bf16[8192,256]{1,0:T(8,128)(2,1)S(1)}, u32[]{:S(2)}, u32[]{:S(2)}) %collective-permute-start) | collective-permute-done | bytes 4194336 | tf_op jit(solution)/shard_map/ppermute | solution.py:32
  103.1 0.0 copy-start.1
  103.1 2.0 copy-done.1
  105.1 0.0 collective-permute-start.1
  105.1 93.6 %collective-permute-done.1 = bf16[8192,256]{1,0:T(8,128)(2,1)} collective-permute-done((bf16[8192,256]{1,0:T(8,128)(2,1)S(1)}, bf16[8192,256]{1,0:T(8,128)(2,1)}, u32[]{:S(2)}, u32[]{:S(2)}) %collective-permute-start.1) | collective-permute-done | bytes 4194336 | tf_op jit(solution)/shard_map/ppermute | solution.py:32
  198.8 0.0 collective-permute-start.2
  198.8 0.0 all-gather.2.cloned.1.call-update
  198.8 0.0 reduce-scatter.2.cloned.1.call-start
  198.9 0.0 copy-start.2
  198.9 0.0 copy-start
  198.9 92.9 %collective-permute-done.2 = bf16[8192,256]{1,0:T(8,128)(2,1)} collective-permute-done((bf16[8192,256]{1,0:T(8,128)(2,1)}, bf16[8192,256]{1,0:T(8,128)(2,1)}, u32[]{:S(2)}, u32[]{:S(2)}) %collective-permute-start.2) | collective-permute-done | bytes 4194336 | tf_op jit(solution)/shard_map/ppermute | solution.py:32
  291.8 4.5 constant_dynamic-update-slice_fusion.7
  296.3 4.5 constant_dynamic-update-slice_fusion.6
  300.8 4.5 constant_dynamic-update-slice_fusion.5
  305.3 4.5 constant_dynamic-update-slice_fusion.4
  309.8 4.5 constant_dynamic-update-slice_fusion.3
  314.3 4.5 constant_dynamic-update-slice_fusion.2
  318.8 0.0 copy-done.2
  318.8 2.4 constant_dynamic-update-slice_fusion.1
  321.2 0.0 copy-done
  321.2 2.3 constant_dynamic-update-slice_fusion
  323.5 0.0 all-gather.2.cloned.1.call-done
  323.5 0.0 copy-start.3
  323.5 34.5 %multiply_convert_fusion = (bf16[8192,1024]{1,0:T(8,128)(2,1)}, f32[8192,1024]{1,0:T(8,128)}) fusion(bf16[1024,1024]{1,0:T(8,128)(2,1)} %all-gather.2.cloned.1.call-done, bf16[8192,2048]{1,0:T(8,128)(2,1)} %constant_dynamic-update-slice_fusion, s32[]{:T(128)S(6)} %select_n.14), kind=kOutput, calls=%fused_computation.9 | convolution fusion | flops 17255366656 | bytes 69206016 | tf_op jit(solution)/shard_map/dot_general | solution.py:39
  358.0 0.0 copy-done.3
  358.0 40.2 %convert_bitcast_fusion = bf16[1024,8192]{0,1:T(8,128)(2,1)} fusion(bf16[1024,1024]{1,0:T(8,128)(2,1)S(1)} %copy-done.3, f32[8192,1024]{1,0:T(8,128)} %get-tuple-element.3, bf16[8192,1024]{1,0:T(8,128)(2,1)} %param.5), kind=kOutput, calls=%fused_computation.10 | convolution fusion | flops 17356029952 | bytes 69206016 | tf_op jit(solution)/shard_map/dot_general | solution.py:43
  398.1 0.0 reduce-scatter.2.cloned.1.call-update
  398.2 278.3 %reduce-scatter.2.cloned.1.call-done = bf16[256,8192]{0,1:T(8,128)(2,1)} async-done(((bf16[1024,8192]{0,1:T(8,128)(2,1)}), bf16[256,8192]{0,1:T(8,128)(2,1)}) %reduce-scatter.2.cloned.1.call-update) | async-done | bytes 4194320 | tf_op jit(solution)/shard_map/reduce_scatter | solution.py:42
Async XLA Ops:
  7.2 316.3 %all-gather.2.cloned.1.call-start = ((), (), s32[]{:S(2)}) async-start(), calls=%async_computation.1 | async-start | bytes 2359296 | tf_op jit(solution)/shard_map/all_gather | solution.py:37
  7.2 95.9 %collective-permute-start = (bf16[8192,256]{1,0:T(8,128)(2,1)}, bf16[8192,256]{1,0:T(8,128)(2,1)S(1)}, u32[]{:S(2)}, u32[]{:S(2)}) collective-permute-start(bf16[8192,256]{1,0:T(8,128)(2,1)} %param.3), channel_id=1, source_target_pairs={{0,1},{1,2},{2,3},{3,0},{4,5},{5,6},{6,7},{7,4},{8,9},{9,10},{10,1... | collective-permute-start | bytes 12582920 | tf_op jit(solution)/shard_map/ppermute | solution.py:32
  103.1 2.0 copy-start.1
  105.1 93.6 %collective-permute-start.1 = (bf16[8192,256]{1,0:T(8,128)(2,1)S(1)}, bf16[8192,256]{1,0:T(8,128)(2,1)}, u32[]{:S(2)}, u32[]{:S(2)}) collective-permute-start(bf16[8192,256]{1,0:T(8,128)(2,1)S(1)} %collective-permute-done), channel_id=1, source_target_pairs={{0,1},{1,2},{2,3},{3,0},{4,5},{5,6},{6,7},{7,4},{8,9},{9,10},{10,1... | collective-permute-start | bytes 12582920 | tf_op jit(solution)/shard_map/ppermute | solution.py:32
  198.8 93.0 %collective-permute-start.2 = (bf16[8192,256]{1,0:T(8,128)(2,1)}, bf16[8192,256]{1,0:T(8,128)(2,1)}, u32[]{:S(2)}, u32[]{:S(2)}) collective-permute-start(bf16[8192,256]{1,0:T(8,128)(2,1)} %collective-permute-done.1), channel_id=1, source_target_pairs={{0,1},{1,2},{2,3},{3,0},{4,5},{5,6},{6,7},{7,4},{8,9},{9,10},{10,1... | collective-permute-start | bytes 12582920 | tf_op jit(solution)/shard_map/ppermute | solution.py:32
  198.8 477.7 %reduce-scatter.2.cloned.1.call-start = ((), (), s32[]{:S(2)}) async-start(), calls=%async_computation.2 | async-start | bytes 20971520 | tf_op jit(solution)/shard_map/reduce_scatter | solution.py:42
  198.9 119.9 %copy-start.2 = (bf16[8192,256]{1,0:T(8,128)(2,1)S(1)}, bf16[8192,256]{1,0:T(8,128)(2,1)}, u32[]{:S(2)}) copy-start(bf16[8192,256]{1,0:T(8,128)(2,1)} %copy-done.1) | copy-start | bytes 12582916
  198.9 122.3 %copy-start = (bf16[8192,256]{1,0:T(8,128)(2,1)S(1)}, bf16[8192,256]{1,0:T(8,128)(2,1)}, u32[]{:S(2)}) copy-start(bf16[8192,256]{1,0:T(8,128)(2,1)} %param.3) | copy-start | bytes 12582916
  323.5 34.5 %copy-start.3 = (bf16[1024,1024]{1,0:T(8,128)(2,1)S(1)}, bf16[1024,1024]{1,0:T(8,128)(2,1)}, u32[]{:S(2)}) copy-start(bf16[1024,1024]{1,0:T(8,128)(2,1)} %all-gather.2.cloned.1.call-done) | copy-start | bytes 6291460
Sparse Core Ops, SparseCore 0:
  198.9 29.0 all-gather.1
  398.3 278.1 reduce-scatter.1
